TPU v7x, 512 devices: a whole 4x4x16 slice. The times are simulated.
512 devices in a mesh: row: 16 (over z_hi, y), col: 32 (over z_lo, x, core).
Axes of the slice: x: 4, y: 4, z: 16 (z_hi: 4, z_lo: 4; z = z_hi * 4 + z_lo), core: 2. Of those that a mesh axis runs over, the one named last changes fastest.
Arguments:
- grad_out: bfloat16 [65536, 512], P(('row', 'col'))
- relu_mask: int32 [65536, 512], P(('row', 'col')), may hold values 0 or 1
- aggregated: bfloat16 [65536, 512], P(('row', 'col')), may hold values from -6 to 6
- weight: bfloat16 [512, 512], replicated, may hold values from -0.25 to 0.25
- adj_blocks: bfloat16 [16, 32, 85, 128, 128], P('row', 'col'), may hold values from 0 to 0.02876383
- block_pos: int32 [16, 32, 85], P('row', 'col'), may hold values from 0 to 511, as said below
- block_live: int32 [16, 32], P('row', 'col'), may hold values from 1 to 85, as said below
Outputs:
- grad_input: bfloat16 [32, 2048, 512], P('col', 'row')
- grad_weight: float32 [512, 512], replicated
- grad_bias: float32 [512], replicated
Inputs may be any that keep to these rules, and one draw needn't show every extreme that they name: `block_pos`: within one tile the 85 slots name different positions; position p is block row p // 16, block column p % 16. `block_live`: some tile uses all 85 slots.
All inputs are finite; a program needn't handle non-finite values. No bound on the sum of `relu_mask` on one device may be relied on, other than what follows from the above.
Results may differ from a plain program's by a relative error of at most 0.005.
Values may be sent and summed in bfloat16 or wider, within the bound.
No kernel may reach another device: no remote copies, remote signals or barrier semaphores. Data moves between devices by JAX's collectives and lax.ppermute only.
A program may use at most 64 MiB of HBM per device.

v0:
```python
import math
import jax
import jax.numpy as jnp
from jax import lax
from jax.sharding import PartitionSpec as P


def body(grad_out, relu_mask, aggregated, weight, adj_blocks, block_pos, block_live):
    rows_dev, feat_dim = grad_out.shape
    grad_pre = grad_out * relu_mask.astype(jnp.bfloat16)
    projected = jnp.einsum(
        "ng,fg->nf", grad_pre, weight, preferred_element_type=jnp.float32
    ).astype(jnp.bfloat16)
    row_block = lax.all_gather(projected, "col", axis=0, tiled=True)
    blocks = adj_blocks[0, 0]
    positions = block_pos[0, 0]
    live_count = block_live[0, 0]
    capacity = blocks.shape[0]
    block_width = blocks.shape[-1]
    tile_cols = lax.axis_size("row") * rows_dev // block_width
    tile_row_count = row_block.shape[0] // block_width
    stacked_tiles = row_block.reshape(tile_row_count, block_width, feat_dim)
    group_size = max((divisor for divisor in range(1, 17) if capacity % divisor == 0))
    group_turns = capacity // group_size
    column_ids = jnp.arange(tile_cols, dtype=jnp.int32)

    def add_group(running_total, turn_index):
        first_slot = turn_index * group_size
        part_blocks = lax.dynamic_slice_in_dim(blocks, first_slot, group_size, 0)
        part_slots = lax.dynamic_slice_in_dim(positions, first_slot, group_size, 0)
        selected_row_set = stacked_tiles[part_slots // tile_cols]
        partial_products = jnp.einsum(
            "kab,kaf->kbf", part_blocks, selected_row_set, preferred_element_type=jnp.float32
        )
        alive = first_slot + jnp.arange(group_size, dtype=jnp.int32) < live_count
        insert_position = ((part_slots % tile_cols)[:, None] == column_ids[None, :]) & alive[
            :, None
        ]
        update = jnp.einsum(
            "lj,lsu->jsu",
            insert_position.astype(jnp.float32),
            partial_products,
            precision=lax.Precision.HIGHEST,
        )
        return (running_total + update, None)

    start_sum = jnp.zeros((tile_cols, block_width, feat_dim), jnp.float32)
    running_total, _ = lax.scan(add_group, start_sum, jnp.arange(group_turns, dtype=jnp.int32))
    column_terms = running_total.reshape(tile_cols * block_width, feat_dim)
    summed = lax.psum_scatter(column_terms, "row", scatter_dimension=0, tiled=True)
    grad_input = summed.astype(jnp.bfloat16).reshape(1, rows_dev, feat_dim)
    weight_terms = jnp.einsum("nf,ng->fg", aggregated, grad_pre, preferred_element_type=jnp.float32)
    bias_terms = jnp.sum(grad_pre.astype(jnp.float32), axis=0)
    factor = 1.0 / math.sqrt(rows_dev * lax.axis_size("row") * lax.axis_size("col"))
    weight_gradient_total, bias_total = lax.psum((weight_terms, bias_terms), ("row", "col"))
    return (grad_input, weight_gradient_total * factor, bias_total * factor)


def solution(mesh):
    return jax.shard_map(
        body,
        mesh=mesh,
        in_specs=(
            P(("row", "col"), None),
            P(("row", "col"), None),
            P(("row", "col"), None),
            P(),
            P("row", "col", None, None, None),
            P("row", "col", None),
            P("row", "col"),
        ),
        out_specs=(P("col", "row", None), P(), P()),
        check_vma=False,
    )
```

profile of v0, /device:TPU:1, one launch (start us, length us, event | category | flops | bytes accessed | tf_op | source)
XLA Modules:
  0.0 523.1 jit_solution(11455040609310705814)
XLA Ops:
  10.2 2.2 convolution_bitcast_fusion
  12.5 73.2 %all-gather.2.cloned.1.call-done = bf16[4096,512]{1,0:T(8,128)(2,1)} async-done(((bf16[128,512]{1,0:T(8,128)(2,1)}), bf16[4096,512]{1,0:T(8,128)(2,1)}) %all-gather.2.cloned.1.call-update) | async-done | bytes 4194320 | tf_op jit(solution)/shard_map/all_gather | solution.py:14
  85.7 228.2 %while.13 = (s32[]{:T(128)}, f32[16,128,512]{2,0,1:T(8,128)}, s32[17]{0:T(128)S(1)}, s32[85]{0:T(128)}, s32[]{:T(128)}, /*index=5*/bf16[85,128,128]{2,1,0:T(8,12...) while((s32[]{:T(128)}, f32[16,128,512]{2,0,1:T(8,128)}, ...), condition=%wide.region_1.2_spmd.clone, body=%wide.region_0.1_spmd.clone.sunk | while | flops 148899120 | bytes 13144451 | solution.py:48
  88.4 2.8 gather_fusion
  91.2 1.3 fusion.25
  93.2 4.5 select_add_fusion.2
  100.4 2.8 gather_fusion
  103.2 1.3 fusion.25
  105.2 6.0 %select_add_fusion.2 = f32[16,128,512]{2,0,1:T(8,128)} fusion(f32[16,128,512]{2,0,1:T(8,128)} %get-tuple-element.214, f32[5,128,512]{2,1,0:T(8,128)S(1)} %fusion.25, pred[]{:T(512)S(6)} %compare.10, s32[5]{0:T(128)S(1)} %get-tuple-element.201, pred[5]{0:T(512)(128)(4,1)S(1)} %add_compare_fusion.2), kind=kOutput, calls=%fused_computation.2.clone.1 | convolution fusion | flops 65011872 | bytes 9699354 | tf_op jit(solution)/shard_map/while/body/eval_jaxpr/lj,lsu->jsu/dot_general | solution.py:39
  113.9 2.8 gather_fusion
  118.7 6.0 %select_add_fusion.2 = f32[16,128,512]{2,0,1:T(8,128)} fusion(f32[16,128,512]{2,0,1:T(8,128)} %get-tuple-element.214, f32[5,128,512]{2,1,0:T(8,128)S(1)} %fusion.25, pred[]{:T(512)S(6)} %compare.10, s32[5]{0:T(128)S(1)} %get-tuple-element.201, pred[5]{0:T(512)(128)(4,1)S(1)} %add_compare_fusion.2), kind=kOutput, calls=%fused_computation.2.clone.1 | convolution fusion | flops 65011872 | bytes 9699354 | tf_op jit(solution)/shard_map/while/body/eval_jaxpr/lj,lsu->jsu/dot_general | solution.py:39
  127.5 2.8 gather_fusion
  132.2 6.0 %select_add_fusion.2 = f32[16,128,512]{2,0,1:T(8,128)} fusion(f32[16,128,512]{2,0,1:T(8,128)} %get-tuple-element.214, f32[5,128,512]{2,1,0:T(8,128)S(1)} %fusion.25, pred[]{:T(512)S(6)} %compare.10, s32[5]{0:T(128)S(1)} %get-tuple-element.201, pred[5]{0:T(512)(128)(4,1)S(1)} %add_compare_fusion.2), kind=kOutput, calls=%fused_computation.2.clone.1 | convolution fusion | flops 65011872 | bytes 9699354 | tf_op jit(solution)/shard_map/while/body/eval_jaxpr/lj,lsu->jsu/dot_general | solution.py:39
  141.0 2.8 gather_fusion
  145.8 6.0 %select_add_fusion.2 = f32[16,128,512]{2,0,1:T(8,128)} fusion(f32[16,128,512]{2,0,1:T(8,128)} %get-tuple-element.214, f32[5,128,512]{2,1,0:T(8,128)S(1)} %fusion.25, pred[]{:T(512)S(6)} %compare.10, s32[5]{0:T(128)S(1)} %get-tuple-element.201, pred[5]{0:T(512)(128)(4,1)S(1)} %add_compare_fusion.2), kind=kOutput, calls=%fused_computation.2.clone.1 | convolution fusion | flops 65011872 | bytes 9699354 | tf_op jit(solution)/shard_map/while/body/eval_jaxpr/lj,lsu->jsu/dot_general | solution.py:39
  154.5 2.8 gather_fusion
  159.3 6.0 %select_add_fusion.2 = f32[16,128,512]{2,0,1:T(8,128)} fusion(f32[16,128,512]{2,0,1:T(8,128)} %get-tuple-element.214, f32[5,128,512]{2,1,0:T(8,128)S(1)} %fusion.25, pred[]{:T(512)S(6)} %compare.10, s32[5]{0:T(128)S(1)} %get-tuple-element.201, pred[5]{0:T(512)(128)(4,1)S(1)} %add_compare_fusion.2), kind=kOutput, calls=%fused_computation.2.clone.1 | convolution fusion | flops 65011872 | bytes 9699354 | tf_op jit(solution)/shard_map/while/body/eval_jaxpr/lj,lsu->jsu/dot_general | solution.py:39
  168.0 2.8 gather_fusion
  172.8 6.0 %select_add_fusion.2 = f32[16,128,512]{2,0,1:T(8,128)} fusion(f32[16,128,512]{2,0,1:T(8,128)} %get-tuple-element.214, f32[5,128,512]{2,1,0:T(8,128)S(1)} %fusion.25, pred[]{:T(512)S(6)} %compare.10, s32[5]{0:T(128)S(1)} %get-tuple-element.201, pred[5]{0:T(512)(128)(4,1)S(1)} %add_compare_fusion.2), kind=kOutput, calls=%fused_computation.2.clone.1 | convolution fusion | flops 65011872 | bytes 9699354 | tf_op jit(solution)/shard_map/while/body/eval_jaxpr/lj,lsu->jsu/dot_general | solution.py:39
  181.5 2.8 gather_fusion
  184.3 1.3 fusion.25
  186.3 6.0 %select_add_fusion.2 = f32[16,128,512]{2,0,1:T(8,128)} fusion(f32[16,128,512]{2,0,1:T(8,128)} %get-tuple-element.214, f32[5,128,512]{2,1,0:T(8,128)S(1)} %fusion.25, pred[]{:T(512)S(6)} %compare.10, s32[5]{0:T(128)S(1)} %get-tuple-element.201, pred[5]{0:T(512)(128)(4,1)S(1)} %add_compare_fusion.2), kind=kOutput, calls=%fused_computation.2.clone.1 | convolution fusion | flops 65011872 | bytes 9699354 | tf_op jit(solution)/shard_map/while/body/eval_jaxpr/lj,lsu->jsu/dot_general | solution.py:39
  195.1 2.8 gather_fusion
  199.8 6.0 %select_add_fusion.2 = f32[16,128,512]{2,0,1:T(8,128)} fusion(f32[16,128,512]{2,0,1:T(8,128)} %get-tuple-element.214, f32[5,128,512]{2,1,0:T(8,128)S(1)} %fusion.25, pred[]{:T(512)S(6)} %compare.10, s32[5]{0:T(128)S(1)} %get-tuple-element.201, pred[5]{0:T(512)(128)(4,1)S(1)} %add_compare_fusion.2), kind=kOutput, calls=%fused_computation.2.clone.1 | convolution fusion | flops 65011872 | bytes 9699354 | tf_op jit(solution)/shard_map/while/body/eval_jaxpr/lj,lsu->jsu/dot_general | solution.py:39
  208.6 2.8 gather_fusion
  213.3 6.0 %select_add_fusion.2 = f32[16,128,512]{2,0,1:T(8,128)} fusion(f32[16,128,512]{2,0,1:T(8,128)} %get-tuple-element.214, f32[5,128,512]{2,1,0:T(8,128)S(1)} %fusion.25, pred[]{:T(512)S(6)} %compare.10, s32[5]{0:T(128)S(1)} %get-tuple-element.201, pred[5]{0:T(512)(128)(4,1)S(1)} %add_compare_fusion.2), kind=kOutput, calls=%fused_computation.2.clone.1 | convolution fusion | flops 65011872 | bytes 9699354 | tf_op jit(solution)/shard_map/while/body/eval_jaxpr/lj,lsu->jsu/dot_general | solution.py:39
  222.1 2.8 gather_fusion
  224.9 1.3 fusion.25
  226.8 6.0 %select_add_fusion.2 = f32[16,128,512]{2,0,1:T(8,128)} fusion(f32[16,128,512]{2,0,1:T(8,128)} %get-tuple-element.214, f32[5,128,512]{2,1,0:T(8,128)S(1)} %fusion.25, pred[]{:T(512)S(6)} %compare.10, s32[5]{0:T(128)S(1)} %get-tuple-element.201, pred[5]{0:T(512)(128)(4,1)S(1)} %add_compare_fusion.2), kind=kOutput, calls=%fused_computation.2.clone.1 | convolution fusion | flops 65011872 | bytes 9699354 | tf_op jit(solution)/shard_map/while/body/eval_jaxpr/lj,lsu->jsu/dot_general | solution.py:39
  235.6 2.8 gather_fusion
  240.3 6.0 %select_add_fusion.2 = f32[16,128,512]{2,0,1:T(8,128)} fusion(f32[16,128,512]{2,0,1:T(8,128)} %get-tuple-element.214, f32[5,128,512]{2,1,0:T(8,128)S(1)} %fusion.25, pred[]{:T(512)S(6)} %compare.10, s32[5]{0:T(128)S(1)} %get-tuple-element.201, pred[5]{0:T(512)(128)(4,1)S(1)} %add_compare_fusion.2), kind=kOutput, calls=%fused_computation.2.clone.1 | convolution fusion | flops 65011872 | bytes 9699354 | tf_op jit(solution)/shard_map/while/body/eval_jaxpr/lj,lsu->jsu/dot_general | solution.py:39
  249.1 2.8 gather_fusion
  253.9 6.0 %select_add_fusion.2 = f32[16,128,512]{2,0,1:T(8,128)} fusion(f32[16,128,512]{2,0,1:T(8,128)} %get-tuple-element.214, f32[5,128,512]{2,1,0:T(8,128)S(1)} %fusion.25, pred[]{:T(512)S(6)} %compare.10, s32[5]{0:T(128)S(1)} %get-tuple-element.201, pred[5]{0:T(512)(128)(4,1)S(1)} %add_compare_fusion.2), kind=kOutput, calls=%fused_computation.2.clone.1 | convolution fusion | flops 65011872 | bytes 9699354 | tf_op jit(solution)/shard_map/while/body/eval_jaxpr/lj,lsu->jsu/dot_general | solution.py:39
  262.6 2.8 gather_fusion
  267.4 6.0 %select_add_fusion.2 = f32[16,128,512]{2,0,1:T(8,128)} fusion(f32[16,128,512]{2,0,1:T(8,128)} %get-tuple-element.214, f32[5,128,512]{2,1,0:T(8,128)S(1)} %fusion.25, pred[]{:T(512)S(6)} %compare.10, s32[5]{0:T(128)S(1)} %get-tuple-element.201, pred[5]{0:T(512)(128)(4,1)S(1)} %add_compare_fusion.2), kind=kOutput, calls=%fused_computation.2.clone.1 | convolution fusion | flops 65011872 | bytes 9699354 | tf_op jit(solution)/shard_map/while/body/eval_jaxpr/lj,lsu->jsu/dot_general | solution.py:39
  276.1 2.8 gather_fusion
  280.9 6.0 %select_add_fusion.2 = f32[16,128,512]{2,0,1:T(8,128)} fusion(f32[16,128,512]{2,0,1:T(8,128)} %get-tuple-element.214, f32[5,128,512]{2,1,0:T(8,128)S(1)} %fusion.25, pred[]{:T(512)S(6)} %compare.10, s32[5]{0:T(128)S(1)} %get-tuple-element.201, pred[5]{0:T(512)(128)(4,1)S(1)} %add_compare_fusion.2), kind=kOutput, calls=%fused_computation.2.clone.1 | convolution fusion | flops 65011872 | bytes 9699354 | tf_op jit(solution)/shard_map/while/body/eval_jaxpr/lj,lsu->jsu/dot_general | solution.py:39
  289.6 2.8 gather_fusion
  292.4 1.3 fusion.25
  294.4 6.0 %select_add_fusion.2 = f32[16,128,512]{2,0,1:T(8,128)} fusion(f32[16,128,512]{2,0,1:T(8,128)} %get-tuple-element.214, f32[5,128,512]{2,1,0:T(8,128)S(1)} %fusion.25, pred[]{:T(512)S(6)} %compare.10, s32[5]{0:T(128)S(1)} %get-tuple-element.201, pred[5]{0:T(512)(128)(4,1)S(1)} %add_compare_fusion.2), kind=kOutput, calls=%fused_computation.2.clone.1 | convolution fusion | flops 65011872 | bytes 9699354 | tf_op jit(solution)/shard_map/while/body/eval_jaxpr/lj,lsu->jsu/dot_general | solution.py:39
  303.1 2.8 gather_fusion
  307.9 6.0 %select_add_fusion.2 = f32[16,128,512]{2,0,1:T(8,128)} fusion(f32[16,128,512]{2,0,1:T(8,128)} %get-tuple-element.214, f32[5,128,512]{2,1,0:T(8,128)S(1)} %fusion.25, pred[]{:T(512)S(6)} %compare.10, s32[5]{0:T(128)S(1)} %get-tuple-element.201, pred[5]{0:T(512)(128)(4,1)S(1)} %add_compare_fusion.2), kind=kOutput, calls=%fused_computation.2.clone.1 | convolution fusion | flops 65011872 | bytes 9699354 | tf_op jit(solution)/shard_map/while/body/eval_jaxpr/lj,lsu->jsu/dot_general | solution.py:39
  313.9 6.5 %copy.10 = f32[16,128,512]{2,1,0:T(8,128)} copy(f32[16,128,512]{2,0,1:T(8,128)} %get-tuple-element.107) | data formatting | bytes 8388608 | tf_op jit(solution)/shard_map/while | solution.py:48
  320.5 122.6 %psum.15 = f32[512]{0:T(512)S(1)} all-reduce(f32[512]{0:T(512)S(1)} %get-tuple-element.153), channel_id=1, replica_groups=mesh['row'=16,'col'=32] {'row','col'}, use_global_device_ids=true, to_apply=%region_5.6 | all-reduce | flops 512 | bytes 4096 | tf_op jit(solution)/shard_map/psum | solution.py:55
  443.7 67.7 %all-reduce.2.cloned.1.call-done = f32[512,512]{0,1:T(8,128)} async-done(((f32[512,512]{0,1:T(8,128)}), f32[512,512]{0,1:T(8,128)}) %all-reduce.2.cloned.1.call-update) | async-done | bytes 1048592 | tf_op jit(solution)/shard_map/psum | solution.py:55
  511.4 1.3 broadcast_multiply_fusion
  512.8 1.3 copy.11
  514.1 1.6 convert_bitcast_fusion
  (111 shorter events, 64.7 us)
Async XLA Ops:
  8.0 1.2 copy-start
  8.0 77.7 %all-gather.2.cloned.1.call-start = ((), (), s32[]{:S(2)}) async-start(), calls=%async_computation.1 | async-start | bytes 4325376 | tf_op jit(solution)/shard_map/all_gather | solution.py:14
  10.2 501.3 %all-reduce.2.cloned.1.call-start = ((), (), s32[]{:S(2)}) async-start(), calls=%async_computation.3 | async-start | bytes 2097152 | tf_op jit(solution)/shard_map/psum | solution.py:55
  12.4 501.6 %reduce-scatter.2.cloned.1.call-start = ((), (), s32[]{:S(2)}) async-start(), calls=%async_computation.2 | async-start | bytes 4456448 | tf_op jit(solution)/shard_map/reduce_scatter | solution.py:50
Sparse Core Ops, SparseCore 0:
  11.6 74.1 all-gather.1
  320.6 151.5 reduce-scatter.1
Sparse Core Ops, SparseCore 1:
  17.6 493.8 all-reduce.1
where the time goes:
time: 525 us; the launch traced here: 523 us
  waiting for transfers between devices  141 us (27%)
  matrix products  126 us (24%)
  blocking collectives  123 us (23%)
  local copies, waits for them, and re-layouts  65 us (12%)
  other arithmetic  41 us (8%)
  between operations  15.5 us (3%)
  loops' own time  11.6 us (2%)
    psum x1, blocking collectives, body(): lax.psum((weight_terms, bias_terms), ('row', 'col'))  123 us
    dot_general x17, matrix products, add_group(): jnp.einsum('lj,lsu->jsu', insert_position.astype(jnp.float32), partial_pr...  101 us
    all_gather x1, waiting for transfers between devices, body(): row_block = lax.all_gather(projected, 'col', axis=0, tiled=True)  73.2 us
    psum x1, waiting for transfers between devices, body(): lax.psum((weight_terms, bias_terms), ('row', 'col'))  67.7 us
    gather x17, local copies, waits for them, and re-layouts, add_group(): selected_row_set = stacked_tiles[part_slots // tile_cols]  47.2 us
    dot_general x17, matrix products, add_group(): jnp.einsum('kab,kaf->kbf', part_blocks, selected_row_set, preferred_eleme...  22.1 us
    select_n x17, other arithmetic, add_group(): part_slots % tile_cols  12.6 us
    select_n x17, other arithmetic, add_group(): selected_row_set = stacked_tiles[part_slots // tile_cols]  12.5 us
  transfers between devices with their start and end apart: 3, of which 2 were waited for; matrix products, arithmetic and copies ran while one was open for 44% of the time, Pallas kernels for 0%

commit v1 on v0

--- a/solution.py
+++ b/solution.py
@@ -52,7 +52,7 @@
     weight_terms = jnp.einsum("nf,ng->fg", aggregated, grad_pre, preferred_element_type=jnp.float32)
     bias_terms = jnp.sum(grad_pre.astype(jnp.float32), axis=0)
     factor = 1.0 / math.sqrt(rows_dev * lax.axis_size("row") * lax.axis_size("col"))
-    weight_gradient_total, bias_total = lax.psum((weight_terms, bias_terms), ("row", "col"))
+    weight_gradient_total, bias_total = lax.psum(lax.psum((weight_terms, bias_terms), "row"), "col")
     return (grad_input, weight_gradient_total * factor, bias_total * factor)
 
 

time: 525 us -> 611 us (1.16)
  waiting for transfers between devices: 141 us -> 233 us
  other arithmetic: 41 us -> 18.7 us
  blocking collectives: 123 us -> 140 us
    psum x1 -> x2, waiting for transfers between devices: 67.7 us -> 208 us  [the longest x1 208 us: body(): lax.psum((weight_terms, bias_terms), 'row')]
    all_gather x1, waiting for transfers between devices: 73.2 us -> 0.03 us  [body(): row_block = lax.all_gather(projected, 'col', axis=0, tiled=True)]
    reduce_scatter x1, waiting for transfers between devices: 0.01 us -> 24.5 us  [body(): lax.psum_scatter(column_terms, 'row', scatter_dimension=0, tiled=True)]
    psum x1 -> x2, blocking collectives: 123 us -> 140 us  [the longest x1 89.3 us: body(): lax.psum(lax.psum((weight_terms, bias_terms), 'row'), 'col')]
    select_n x17, other arithmetic: 12.6 us -> 1.42 us  [add_group(): part_slots % tile_cols]
    select_n x17, other arithmetic: 12.5 us -> 1.41 us  [add_group(): selected_row_set = stacked_tiles[part_slots // tile_cols]]
  transfers between devices with their start and end apart: 3 -> 4, of which waited for: 2 -> 2; matrix products, arithmetic and copies ran while one was open for 44% -> 34% of each run, Pallas kernels for 0% -> 0%
where the time goes in v1:
time: 611 us; the launch traced here: 610 us
  waiting for transfers between devices  233 us (38%)
  blocking collectives  140 us (23%)
  matrix products  126 us (21%)
  local copies, waits for them, and re-layouts  65.1 us (11%)
  other arithmetic  18.7 us (3%)
  between operations  15.6 us (3%)
  loops' own time  11.6 us (2%)
    psum x1, waiting for transfers between devices, body(): lax.psum((weight_terms, bias_terms), 'row')  208 us
    dot_general x17, matrix products, add_group(): jnp.einsum('lj,lsu->jsu', insert_position.astype(jnp.float32), partial_pr...  101 us
    psum x1, blocking collectives, body(): lax.psum(lax.psum((weight_terms, bias_terms), 'row'), 'col')  89.3 us
    psum x1, blocking collectives, body(): lax.psum((weight_terms, bias_terms), 'row')  50.3 us
    gather x17, local copies, waits for them, and re-layouts, add_group(): selected_row_set = stacked_tiles[part_slots // tile_cols]  47.3 us
    reduce_scatter x1, waiting for transfers between devices, body(): lax.psum_scatter(column_terms, 'row', scatter_dimension=0, tiled=True)  24.5 us
    dot_general x17, matrix products, add_group(): jnp.einsum('kab,kaf->kbf', part_blocks, selected_row_set, preferred_eleme...  22.1 us
  transfers between devices with their start and end apart: 4, of which 2 were waited for; matrix products, arithmetic and copies ran while one was open for 34% of the time, Pallas kernels for 0%

profile of v1, /device:TPU:1, one launch (start us, length us, event | category | flops | bytes accessed | tf_op | source)
XLA Modules:
  0.0 609.9 jit_solution(9628883099548400500)
XLA Ops:
  9.2 2.2 convolution_bitcast_fusion
  12.5 208.3 %all-reduce.3.cloned.1.call-done = f32[512,512]{0,1:T(8,128)} async-done(((f32[512,512]{0,1:T(8,128)}), f32[512,512]{0,1:T(8,128)}) %all-reduce.3.cloned.1.call-update) | async-done | bytes 1048592 | tf_op jit(solution)/shard_map/psum | solution.py:55
  221.0 205.9 %while.13 = (s32[]{:T(128)}, f32[16,128,512]{2,0,1:T(8,128)}, s32[17]{0:T(128)S(1)}, s32[85]{0:T(128)S(1)}, s32[]{:T(128)}, /*index=5*/bf16[85,128,128]{2,1,0:T(...) while((s32[]{:T(128)}, f32[16,128,512]{2,0,1:T(8,128)}, ...), condition=%wide.region_1.2_spmd.clone, body=%wide.region_0.1_spmd.clone.sunk | while | flops 148899120 | bytes 13144451 | solution.py:48
  222.4 2.8 gather_fusion
  227.2 4.5 select_add_fusion.2
  233.0 2.8 gather_fusion
  237.8 6.0 select_add_fusion.2
  245.2 2.8 gather_fusion
  250.0 6.0 select_add_fusion.2
  257.4 2.8 gather_fusion
  262.2 6.0 select_add_fusion.2
  269.6 2.8 gather_fusion
  272.4 1.3 fusion.25
  274.4 6.0 select_add_fusion.2
  281.8 2.8 gather_fusion
  286.6 6.0 select_add_fusion.2
  294.1 2.8 gather_fusion
  298.8 6.0 select_add_fusion.2
  306.3 2.8 gather_fusion
  311.0 6.0 select_add_fusion.2
  318.5 2.8 gather_fusion
  321.3 1.3 fusion.25
  323.2 6.0 select_add_fusion.2
  330.7 2.8 gather_fusion
  335.4 6.0 select_add_fusion.2
  342.9 2.8 gather_fusion
  345.7 1.3 fusion.25
  347.6 6.0 select_add_fusion.2
  355.1 2.8 gather_fusion
  357.9 1.3 fusion.25
  359.8 6.0 select_add_fusion.2
  367.3 2.8 gather_fusion
  372.0 6.0 select_add_fusion.2
  379.5 2.8 gather_fusion
  384.2 6.0 select_add_fusion.2
  391.6 2.8 gather_fusion
  396.4 6.0 select_add_fusion.2
  403.9 2.8 gather_fusion
  408.6 6.0 select_add_fusion.2
  416.1 2.8 gather_fusion
  420.8 6.0 select_add_fusion.2
  426.8 6.5 %copy.10 = f32[16,128,512]{2,1,0:T(8,128)} copy(f32[16,128,512]{2,0,1:T(8,128)} %get-tuple-element.107) | data formatting | bytes 8388608 | tf_op jit(solution)/shard_map/while | solution.py:48
  433.4 50.3 %psum.30 = f32[512]{0:T(512)S(1)} all-reduce(f32[512]{0:T(512)S(1)} %get-tuple-element.153), channel_id=1, replica_groups=mesh['row'=16,'col'=32] {'row'}, use_global_device_ids=true, to_apply=%region_6.7 | all-reduce | flops 512 | bytes 4096 | tf_op jit(solution)/shard_map/psum | solution.py:55
  483.7 89.3 %psum.31 = f32[512]{0:T(512)S(1)} all-reduce(f32[512]{0:T(512)S(1)} %psum.30), channel_id=1, replica_groups=mesh['row'=16,'col'=32] {'col'}, use_global_device_ids=true, to_apply=%region_7.8 | all-reduce | flops 512 | bytes 4096 | tf_op jit(solution)/shard_map/psum | solution.py:55
  573.6 1.3 broadcast_multiply_fusion
  575.0 1.3 copy.11
  576.3 24.5 %reduce-scatter.2.cloned.1.call-done = f32[128,512]{1,0:T(8,128)} async-done(((f32[2048,512]{1,0:T(8,128)}), f32[128,512]{1,0:T(8,128)}) %reduce-scatter.2.cloned.1.call-update) | async-done | bytes 262160 | tf_op jit(solution)/shard_map/reduce_scatter | solution.py:50
  600.8 1.6 convert_bitcast_fusion
  (117 shorter events, 43.8 us)
Async XLA Ops:
  8.0 3.5 copy-start
  8.0 213.0 %copy-start.1 = (s32[1,1,85]{2,1,0:T(1,128)S(1)}, s32[1,1,85]{2,1,0:T(1,128)}, u32[]{:S(2)}) copy-start(s32[1,1,85]{2,1,0:T(1,128)} %param.14) | copy-start | bytes 1024
  8.0 212.8 %all-reduce.3.cloned.1.call-start = ((), (), s32[]{:S(2)}) async-start(), calls=%async_computation.3 | async-start | bytes 2097152 | tf_op jit(solution)/shard_map/psum | solution.py:55
  11.4 209.5 %all-gather.2.cloned.1.call-start = ((), (), s32[]{:S(2)}) async-start(), calls=%async_computation.1 | async-start | bytes 4325376 | tf_op jit(solution)/shard_map/all_gather | solution.py:14
  12.5 561.2 %all-reduce.5.cloned.1.call-start = ((), (), s32[]{:S(2)}) async-start(), calls=%async_computation.4 | async-start | bytes 2097152 | tf_op jit(solution)/shard_map/psum | solution.py:55
  220.9 379.9 %reduce-scatter.2.cloned.1.call-start = ((), (), s32[]{:S(2)}) async-start(), calls=%async_computation.2 | async-start | bytes 4456448 | tf_op jit(solution)/shard_map/reduce_scatter | solution.py:50
Sparse Core Ops, SparseCore 0:
  12.4 208.4 all-reduce.2
  433.5 167.2 reduce-scatter.1
Sparse Core Ops, SparseCore 1:
  14.8 77.3 all-gather.1
  221.0 311.9 all-reduce.4
